TPU v7x, 128 devices: a whole 4x4x4 slice. The times are simulated.
128 devices in a mesh: row: 4 (over y_lo, core), col: 32 (over y_hi, x, z).
Axes of the slice: x: 4, y: 4 (y_hi: 2, y_lo: 2; y = y_hi * 2 + y_lo), z: 4, core: 2. Of those that a mesh axis runs over, the one named last changes fastest.
Arguments:
- row_coords: bfloat16 [3, 4096, 512], P(None, ('row', 'col')), may hold values from -10 to 10, as said below
- col_coords: bfloat16 [3, 32768, 512], P(None, 'col'), may hold values from -10 to 10, as said below
- start_block: float32 [32768, 64], P('col'), may hold values from -0.03125 to 0.03125
Outputs:
- basis: float32 [4096, 64], P('row')
- image: float32 [32768, 64], P('col')
Inputs may be any that keep to these rules, and one draw needn't show every extreme that they name: `row_coords`: coordinates of frames of one molecule in varying conformations. `col_coords`: coordinates of frames of the same molecule in varying conformations.
All inputs are finite; a program needn't handle non-finite values.
Results may differ from a plain program's by a relative error of at most 0.0073.
Values may be sent and summed in bfloat16 or wider, within the bound.
No kernel may reach another device: no remote copies, remote signals or barrier semaphores. Data moves between devices by JAX's collectives and lax.ppermute only.
A program may use at most 128 MiB of HBM per device.

v0:
```python
import functools

import jax
import jax.numpy as jnp
from jax import lax
from jax.experimental import pallas as pl
from jax.experimental.pallas import tpu as pltpu
from jax.sharding import PartitionSpec as P


ATOMS = 512
NEWTON = 8
K = 64
TR = 128
TC = 512
NC = 256
RF = 4096
CF = 32768
HIGHEST = lax.Precision.HIGHEST
OFFSETS = (0, -1, 1, 2)


def centred(coords):
    wide = coords.astype(jnp.float32)
    return wide - jnp.sum(wide, axis=-1, keepdims=True) * (1.0 / ATOMS)


def column_kernel(coords, out, norm):
    total = None
    for k in range(3):
        c = centred(coords[k]).astype(jnp.bfloat16)
        out[k] = c
        w = c.astype(jnp.float32)
        part = jnp.sum(w * w, axis=1, keepdims=True)
        total = part if total is None else total + part
    spread = jnp.broadcast_to(total * (2.0 / ATOMS), (total.shape[0], 128))
    norm[...] = jnp.transpose(spread)[0:8, :]


def column_call(coords):
    frames, step = coords.shape[1], 256
    block = pl.BlockSpec((3, step, ATOMS), lambda i: (0, i, 0))
    return pl.pallas_call(
        column_kernel,
        grid=(frames // step,),
        in_specs=[block],
        out_specs=[block, pl.BlockSpec((8, step), lambda i: (0, i))],
        out_shape=[
            jax.ShapeDtypeStruct(coords.shape, jnp.bfloat16),
            jax.ShapeDtypeStruct((8, frames), jnp.float32),
        ],
        compiler_params=pltpu.CompilerParams(dimension_semantics=("arbitrary",), vmem_limit_bytes=8 << 20),
        cost_estimate=pl.CostEstimate(flops=10 * 3 * frames * ATOMS, bytes_accessed=6 << 20, transcendentals=0),
        name="columns",
    )(pltpu.with_memory_space_constraint(coords, pltpu.HBM))


def pair_kernel(mine, other, out):
    for k in range(3):
        for i, ref in enumerate((mine, other)):
            c = centred(ref[k]).astype(jnp.bfloat16).astype(jnp.float32)
            out[k, 32 * i : 32 * i + 32, :] = (c * (4.0 / ATOMS)).astype(jnp.bfloat16)


def line_kernel(p0, p1, p2, p3, out, sent, sem):
    for i, ref in enumerate((p0, p1, p2, p3)):
        out[:, 64 * i : 64 * i + 64, :] = ref[...]
    copy = pltpu.make_async_copy(out, sent, sem)
    copy.start()
    copy.wait()


def line_call(pieces):
    vmem = pl.BlockSpec(memory_space=pltpu.VMEM)
    shape = (3, 256, ATOMS)
    return pl.pallas_call(
        line_kernel,
        out_shape=[jax.ShapeDtypeStruct(shape, jnp.bfloat16), pltpu.HBM(shape, jnp.bfloat16)],
        in_specs=[vmem] * 4,
        out_specs=[vmem, pl.BlockSpec(memory_space=pltpu.HBM)],
        scratch_shapes=[pltpu.SemaphoreType.DMA],
        compiler_params=pltpu.CompilerParams(vmem_limit_bytes=8 << 20),
        name="line",
    )(*pieces)


def newton_slice(p, u):
    def g(i, j):
        return p[0][i] * p[0][j] + p[1][i] * p[1][j] + p[2][i] * p[2][j]

    g00, g11, g22, g01, g02 = g(0, 0), g(1, 1), g(2, 2), g(0, 1), g(0, 2)
    c0 = p[1][1] * p[2][2] - p[2][1] * p[1][2]
    c1 = p[2][1] * p[0][2] - p[0][1] * p[2][2]
    c2 = p[0][1] * p[1][2] - p[1][1] * p[0][2]
    det = p[0][0] * c0 + p[1][0] * c1 + p[2][0] * c2
    pair = g11 + g22
    q = g00 + pair
    minors = (g00 * pair - g01 * g01 - g02 * g02) + (c0 * c0 + c1 * c1 + c2 * c2)
    twice = det + det
    x = u
    for _ in range(NEWTON):
        a = x * x - q
        x = (a * (0.75 * a + q) + minors) / (a * x - twice)
    return u - x


def dist_kernel(ns, *refs):
    rows = refs[:ns]
    cols, cn, sw = refs[ns : ns + 3]
    outs, t_out = refs[ns + 3 : ns + 5], refs[ns + 5]
    bufs, rn, kept, sems = refs[ns + 6 : ns + 8], refs[ns + 8], refs[ns + 9 : ns + 11], refs[ns + 11]
    nb = rn.shape[0]
    per = nb // ns
    ct = pl.program_id(0)
    last = pl.num_programs(0) - 1

    def frames(rb):
        r = (rb % per) * TR
        return rows[rb // per][:, r : r + TR, :]

    def products(rb, at, buf, units):
        c0 = pl.multiple_of(at * TC, TC)
        lhs = frames(rb).reshape(3 * TR, ATOMS)
        for b, n in units:
            buf[b, :, n * 256 : n * 256 + 256] = lax.dot_general(
                lhs, cols[b, pl.ds(c0 + n * 256, 256), :], (((1,), (1,)), ((), ())), preferred_element_type=jnp.float32
            )

    def newton(rb, buf, slices):
        for r, c in slices:
            p = [[buf[b, a * TR + r : a * TR + r + 16, c : c + 128] for b in range(3)] for a in range(3)]
            u = rn[rb, r : r + 16] + cn[0:1, c : c + 128]
            d = newton_slice(p, u)
            h = d.astype(jnp.bfloat16)
            kept[0][ct, rb * TR + r : rb * TR + r + 16, c : c + 128] = h
            kept[1][ct, rb * TR + r : rb * TR + r + 16, c : c + 128] = (d - h.astype(jnp.float32)).astype(jnp.bfloat16)

    def stores(at, rb):
        rows_at = pl.ds(rb * TR, TR)
        return [
            pltpu.make_async_copy(
                kept[i].at[at, rows_at, :], outs[i].at[rows_at, pl.ds(pl.multiple_of(at * TC, TC), TC)], sems.at[i, at, rb]
            )
            for i in range(2)
        ]

    def panel(rb):
        at = slice(rb * TR, rb * TR + TR)
        w = sw[:, pl.ds(pl.multiple_of(ct * TC, TC), TC)]
        dims = (((1,), (1,)), ((), ()))
        t_out[at, :] += lax.dot_general(
            kept[0][ct, at, :], w, dims, preferred_element_type=jnp.float32
        ) + lax.dot_general(kept[1][ct, at, :], w, dims, preferred_element_type=jnp.float32)

    units = [(b, n) for n in range(TC // 256) for b in range(3)]
    slices = [(r, c) for r in range(0, TR, 16) for c in range(0, TC, 128)]
    share = -(-len(slices) // len(units))

    @pl.when(ct == 0)
    def _():
        t_out[...] = jnp.zeros_like(t_out)
        for rb in range(nb):
            w = frames(rb).astype(jnp.float32)
            n = jnp.sum(jnp.sum(w * w, axis=0), axis=1, keepdims=True) * (2.0 * ATOMS / 16.0)
            rn[rb] = jnp.broadcast_to(n, (TR, 128))
        products(0, 0, bufs[0], units)

    for rb in range(nb):
        after, at = (rb + 1, ct) if rb + 1 < nb else (0, jnp.minimum(ct + 1, last))

        @pl.when(ct <= last)
        def _(rb=rb, after=after, at=at):
            for i in range(len(units)):
                newton(rb, bufs[rb % 2], slices[i * share : (i + 1) * share])
                products(after, at, bufs[(rb + 1) % 2], units[i : i + 1])
                if i == 2 and rb > 0:
                    panel(rb - 1)

        for copy in stores(ct, rb):
            copy.start()

    panel(nb - 1)

    @pl.when(ct == last)
    def _():
        for at in range(sems.shape[1]):
            for rb in range(nb):
                for copy in stores(at, rb):
                    copy.wait()


def whole(a):
    return pl.BlockSpec(a.shape, lambda *_: (0,) * a.ndim)


def dist_call(sources, cols, cn, sw):
    nc = cols.shape[1]
    r = sum(a.shape[1] for a in sources)
    return pl.pallas_call(
        functools.partial(dist_kernel, len(sources)),
        grid=(nc // TC,),
        in_specs=[whole(a) for a in sources]
        + [whole(cols), pl.BlockSpec((8, TC), lambda c: (0, c)), whole(sw)],
        out_specs=[
            pl.BlockSpec(memory_space=pltpu.HBM),
            pl.BlockSpec(memory_space=pltpu.HBM),
            pl.BlockSpec((r, 256), lambda c: (0, 0)),
        ],
        out_shape=[
            pltpu.HBM((r, nc), jnp.bfloat16),
            pltpu.HBM((r, nc), jnp.bfloat16),
            jax.ShapeDtypeStruct((r, 256), jnp.float32),
        ],
        scratch_shapes=[
            pltpu.VMEM((3, 3 * TR, TC), jnp.float32),
            pltpu.VMEM((3, 3 * TR, TC), jnp.float32),
            pltpu.VMEM((r // TR, TR, 128), jnp.float32),
            pltpu.VMEM((nc // TC, r, TC), jnp.bfloat16),
            pltpu.VMEM((nc // TC, r, TC), jnp.bfloat16),
            pltpu.SemaphoreType.DMA((2, nc // TC, r // TR)),
        ],
        compiler_params=pltpu.CompilerParams(dimension_semantics=("arbitrary",), vmem_limit_bytes=20 << 20),
        cost_estimate=pl.CostEstimate(
            flops=r * nc * 9 * 2 * ATOMS, bytes_accessed=8 << 20, transcendentals=r * nc * NEWTON
        ),
    )(*sources, cols, cn, sw)


PIECES = [(dy, i, o) for dy in range(2) for i in range(4) for o in range(4)]
CHUNK_START = (0, 256, 768)


def place(dy, i, o):
    return (o + 1) // 2, (o == 2) * 256 + (i * 2 + dy) * 32


def owner_of(dy, i, o):
    me, core = lax.axis_index("col"), lax.axis_index("row") % 2
    y, x, z = me // 16, (me // 4) % 4, me % 4
    dx = OFFSETS[o] + core * (OFFSETS[i] - OFFSETS[o])
    dz = OFFSETS[i] + core * (OFFSETS[o] - OFFSETS[i])
    return ((y + dy) % 2) * 16 + ((x + dx + 4) % 4) * 4 + (z + dz + 4) % 4


def lanes(shape):
    return lax.broadcasted_iota(jnp.int32, shape, len(shape) - 1)


def pack_kernel(t0, t1, t2, bm, out):
    ts = (t0, t1, t2)
    lane16, lane8 = lanes((16, 128)), lanes((8, 128))
    means = jnp.broadcast_to(bm[...], (8, 128))
    for piece in PIECES:
        dest = owner_of(*piece)
        chunk, at = place(*piece)
        full, sums = [], []
        for r in (at, at + 16):
            t = ts[chunk][r : r + 16, 0:128]
            full.append(t + pltpu.roll(t, 64, 1))
            sums.append(ts[chunk][r : r + 16, 128:256])
        out[dest, 0:16, :] = jnp.where(lane16 < 64, full[0], full[1])
        ext = jnp.where(lane8 < 16, sums[0][0:8], sums[0][8:16])
        ext = jnp.where(lane8 < 32, ext, sums[1][0:8])
        ext = jnp.where(lane8 < 48, ext, sums[1][8:16])
        out[dest, 16:24, :] = jnp.where(lane8 < 64, ext, means)


def owner_kernel(got, out):
    lane = lanes((8, 128))

    def spread(ext):
        one = lambda k: jnp.broadcast_to(ext[:, k : k + 1], (8, 128))
        return jnp.where(lane < 64, one(0), one(32)), jnp.where(lane < 64, one(16), one(48))

    zero = jnp.zeros((8, 128), jnp.float32)
    a, b, e = zero, zero, zero
    for src in range(got.shape[0]):
        ext = got[src, 16:24, :]
        bm = jnp.where(lane < 64, pltpu.roll(ext, 64, 1), ext)
        r0, r1 = spread(ext)
        a = a + (got[src, 0:8, :] + r0 * bm)
        b = b + (got[src, 8:16, :] + r1 * bm)
        e = e + ext
    bm = jnp.where(lane < 64, pltpu.roll(e, 64, 1), e) * (1.0 / got.shape[0])
    r0, r1 = spread(e)
    a = a - r0 * bm
    b = b - r1 * bm
    sub = lax.broadcasted_iota(jnp.int32, (8, 128), 0)
    y = jnp.sum(r0 * a + r1 * b, axis=0, keepdims=True)
    tot = jnp.sum(r0 + r1, axis=0, keepdims=True)
    ext = jnp.where(sub == 0, jnp.broadcast_to(y, (8, 128)), jnp.broadcast_to(tot, (8, 128)))
    for dst in range(got.shape[0]):
        out[dst, 0:8, :] = a
        out[dst, 8:16, :] = b
        out[dst, 16:24, :] = ext


def panel_kernel(got, left, tc_out, stat, arr):
    n = got.shape[0]
    lane1 = lanes((1, 128))

    def both(v):
        return v + pltpu.roll(v, 64, 1)

    total = jnp.sum(jnp.sum(got[:, 0:16, :], axis=0), axis=0, keepdims=True)
    mean = both(total) * (1.0 / (32 * n))
    ext = jnp.sum(got[:, 16:24, :], axis=0)
    y, rows = both(ext[0:1]), both(ext[1:2])
    x = got[:, 0:16, :] - mean
    flat = x.reshape(n * 16, 128)
    g = lax.dot_general(flat, flat, (((0,), (0,)), ((), ())), precision=HIGHEST, preferred_element_type=jnp.float32)
    stat[0:64, :] = g[0:64, :] + pltpu.roll(g[64:128, :], 64, 1)
    sub = lax.broadcasted_iota(jnp.int32, (8, 128), 0)
    tile = jnp.where(sub == 0, mean, jnp.where(sub == 1, y, rows))
    stat[64:72, :] = jnp.broadcast_to(tile, (8, 128))
    for b in range(n):
        tc_out[b * 32 : b * 32 + 16, :] = x[b, :, 0:64]
        tc_out[b * 32 + 16 : b * 32 + 32, :] = x[b, :, 64:128]
    for piece in PIECES:
        src = owner_of(*piece)
        t = got[src, 0:16, :] - mean
        chunk, r = place(*piece)
        r += CHUNK_START[chunk]
        arr[r : r + 16, :] = t
        arr[r + 16 : r + 32, :] = pltpu.roll(t, 64, 1)
    pt = jnp.transpose(arr[...])[0:64, :]
    h = pt.astype(jnp.bfloat16)
    left[0:64, :] = h
    left[64:128, :] = (pt - h.astype(jnp.float32)).astype(jnp.bfloat16)
    left[128:144, :] = jnp.ones((16, pt.shape[1]), jnp.bfloat16)


def image_kernel(me, left, h0, l0, h1, l1, h2, l2, *refs):
    outs, late, sems = refs[:4], refs[4], refs[5]
    k = pl.program_id(0)
    copies = [pltpu.make_async_copy(ref, late.at[i], sems.at[i]) for i, ref in enumerate((h2, l2))]

    @pl.when(k == 0)
    def _():
        for copy in copies:
            copy.start()

    acc = jnp.zeros((144, NC), jnp.float32)
    for at, refs in zip(CHUNK_START, ((h0, l0), (h1, l1))):
        for ref in refs:
            acc += jnp.dot(left[:, at : at + ref.shape[0]], ref[...], preferred_element_type=jnp.float32)

    @pl.when(k == 0)
    def _():
        for copy in copies:
            copy.wait()

    mine = pl.ds(pl.multiple_of((me[0] ^ k) * NC, NC), NC)
    for i in range(2):
        acc += jnp.dot(left[:, CHUNK_START[2] :], late[i, :, mine], preferred_element_type=jnp.float32)
    for j in range(4):

        @pl.when(k == j)
        def _(j=j):
            outs[j][0:64, :] = acc[0:64] + acc[64:128]
            outs[j][64:72, :] = acc[128:136]


def image_call(me, left, chunks):
    flat = [a for c in chunks for a in c[:2]]
    flat[4:] = [pltpu.with_memory_space_constraint(a, pltpu.HBM) for a in flat[4:]]
    spec = lambda a: pl.BlockSpec((a.shape[0], NC), lambda k, me: (0, me[0] ^ k))
    hbm = pl.BlockSpec(memory_space=pltpu.HBM)
    return pl.pallas_call(
        image_kernel,
        grid_spec=pltpu.PrefetchScalarGridSpec(
            num_scalar_prefetch=1,
            grid=(4,),
            in_specs=[pl.BlockSpec(left.shape, lambda k, me: (0, 0))] + [spec(a) for a in flat[:4]] + [hbm] * 2,
            out_specs=[pl.BlockSpec((72, NC), lambda k, me: (0, 0))] * 4,
            scratch_shapes=[pltpu.VMEM((2, *flat[4].shape), jnp.bfloat16), pltpu.SemaphoreType.DMA((2,))],
        ),
        out_shape=[jax.ShapeDtypeStruct((72, NC), jnp.float32)] * 4,
        compiler_params=pltpu.CompilerParams(dimension_semantics=("arbitrary",), vmem_limit_bytes=16 << 20),
        cost_estimate=pl.CostEstimate(flops=2 * 2 * 256 * 1024 * 1024, bytes_accessed=5 << 20, transcendentals=0),
        name="image",
    )(me, left, *flat)


def factor_kernel(s0, s1, s2, s3, m_out, d_out):
    stats = (s0, s1, s2, s3)

    def total(lo, hi):
        return (s0[lo:hi, :] + s1[lo:hi, :]) + (s2[lo:hi, :] + s3[lo:hi, :])

    mean = total(64, 65) * 0.25
    offs = [s[64:65, :] - mean for s in stats]
    y = total(65, 66) - mean * total(66, 67)
    sub = lax.broadcasted_iota(jnp.int32, (8, 128), 0)
    deltas = jnp.zeros((8, 128), jnp.float32)
    for k in range(4):
        deltas = jnp.where(sub == k, offs[k], deltas)
    d_out[...] = jnp.where(sub == 4, y * (1.0 / CF), deltas)
    outer = lax.dot_general(
        deltas, deltas, (((0,), (0,)), ((), ())), precision=HIGHEST, preferred_element_type=jnp.float32
    )
    gram = (total(0, 64) + outer[0:64, :] * (RF // 4)) * (1.0 / (16 * RF))
    lane = lanes((64, 128))
    row = lax.broadcasted_iota(jnp.int32, (64, 128), 0)
    a = jnp.where(lane < 64, gram, jnp.where(lane - 64 == row, 1.0, 0.0))
    tiles = [a[8 * t : 8 * t + 8, :] for t in range(8)]
    eighth = lax.broadcasted_iota(jnp.int32, (8, 128), 0)
    for t in range(8):
        cols = [[jnp.broadcast_to(tiles[i][:, 8 * t + j : 8 * t + j + 1], (8, 128)) for i in range(t, 8)] for j in range(8)]
        rest = tiles[t:]
        for j in range(8):
            spread = lambda v: jnp.broadcast_to(v[j : j + 1, :], (8, 128))
            pivot = spread(cols[j][0])
            inv = 1.0 / pivot
            row_j = spread(rest[0])
            m_out[8 * t + j : 8 * t + j + 1, :] = (row_j * (lax.rsqrt(pivot) * -0.25))[0:1, :]
            below = [v * inv for v in cols[j]]
            below[0] = jnp.where(eighth > j, below[0], 0.0)
            for l in range(j + 1, 8):
                top = spread(cols[l][0])
                cols[l] = [v - m * top for v, m in zip(cols[l], below)]
            rest = [v - m * row_j for v, m in zip(rest, below)]
        tiles[t:] = rest


def join_kernel(w, g1, g2, g3, m, d, out):
    parts = (w[0:64] + g1[0:64]) + (g2[0:64] + g3[0:64])
    sub = lax.broadcasted_iota(jnp.int32, (8, NC), 0)
    sums = jnp.where(sub == 4, -1.0, 0.0)
    for k, ref in enumerate((w, g1, g2, g3)):
        sums = jnp.where(sub == k, ref[64:72], sums)
    add = lax.dot_general(
        d[...], sums, (((0,), (0,)), ((), ())), precision=HIGHEST, preferred_element_type=jnp.float32
    )
    inv = pltpu.roll(m[...], 64, 1)[:, 0:64]
    res = jnp.dot(inv, parts + add[0:64], precision=HIGHEST, preferred_element_type=jnp.float32)
    out[...] = (res * (-0.25 / RF**0.5)).astype(jnp.bfloat16)


def basis_kernel(tc, m, d, out):
    inv = pltpu.roll(m[...], 64, 1)[:, 0:64]
    x = tc[...] + d[0:1, 0:64]
    out[...] = lax.dot_general(
        inv, x, (((1,), (1,)), ((), ())), precision=HIGHEST, preferred_element_type=jnp.float32
    )


def spread_kernel(i0, i1, i2, i3, out):
    me = lax.axis_index("row")
    for k, ref in enumerate((i0, i1, i2, i3)):
        at = pl.multiple_of((me ^ k) * NC, NC)
        out[:, pl.ds(at, NC)] = ref[...].astype(jnp.float32)


def call(kernel, outs, *args, scratch=(), **kw):
    return pl.pallas_call(
        kernel,
        out_shape=outs,
        in_specs=[pl.BlockSpec(memory_space=pltpu.VMEM)] * len(args),
        out_specs=jax.tree.map(lambda _: pl.BlockSpec(memory_space=pltpu.VMEM), outs),
        scratch_shapes=scratch,
        compiler_params=pltpu.CompilerParams(vmem_limit_bytes=8 << 20),
        **kw,
    )(*args)


def index(core, lo, y, x, z):
    return (lo * 2 + core) * 32 + ((y % 2) * 4 + x % 4) * 4 + z % 4


DEVICES = [(c, w, y, x, z) for c in range(2) for w in range(2) for y in range(2) for x in range(4) for z in range(4)]


def shift(a, dy=0, inner=0, outer=0):
    pairs = []
    for c, w, y, x, z in DEVICES:
        dx, dz = (inner, outer) if c else (outer, inner)
        pairs.append((index(c, w, y, x, z), index(c, w, y + dy, x + dx, z + dz)))
    return lax.ppermute(a, ("row", "col"), pairs)


def swap(a, k):
    return lax.ppermute(a, "row", [(r, r ^ k) for r in range(4)])


def from_three(a, axis):
    return [shift(a, **{axis: -o}) for o in OFFSETS[1:]]


def body(row_coords, col_coords, start_block):
    f32 = jnp.float32
    other = shift(row_coords, dy=1)
    cols, cn = column_call(col_coords)
    pair = call(pair_kernel, jax.ShapeDtypeStruct((3, 64, ATOMS), jnp.bfloat16), row_coords, other)
    line, sent = line_call([pair, *from_three(pair, "inner")])
    far = []
    for o in OFFSETS[1:]:
        far.append(shift(sent, outer=-o))

    start = start_block.T
    block_mean = jnp.mean(start, axis=1)
    start = start - block_mean[:, None]
    start_hi = lax.reduce_precision(start, 8, 7)
    ones = jnp.ones((128, start.shape[1]), jnp.bfloat16)
    sw = jnp.concatenate([start_hi.astype(jnp.bfloat16), (start - start_hi).astype(jnp.bfloat16), ones], axis=0)
    bm = jnp.concatenate([block_mean, block_mean])[None, :]

    chunks = []
    for rows in ([line], far[:2], far[2:]):
        chunks.append(dist_call(rows, cols, cn, sw))
    n = lax.axis_size("col")
    packed = jax.ShapeDtypeStruct((n, 24, 128), f32)
    sent = call(pack_kernel, packed, *(c[2] for c in chunks), bm)
    got = lax.all_to_all(sent, "col", 0, 0, tiled=True)
    totals = call(owner_kernel, packed, got)
    got = lax.all_to_all(totals, "col", 0, 0, tiled=True)
    left, tc, stat = call(
        panel_kernel,
        (
            jax.ShapeDtypeStruct((144, 32 * n), jnp.bfloat16),
            jax.ShapeDtypeStruct((32 * n, K), f32),
            jax.ShapeDtypeStruct((72, 128), f32),
        ),
        got,
        scratch=[pltpu.VMEM((32 * n, 128), f32)],
    )
    me = lax.axis_index("row").reshape(1)
    stats = [stat]
    for k in (1, 2, 3):
        stats.append(swap(stat, k))
    partial = image_call(me, left, chunks)
    arrived = [partial[0], *(swap(partial[k], k) for k in (1, 2, 3))]
    m, d = call(
        factor_kernel, (jax.ShapeDtypeStruct((64, 128), f32), jax.ShapeDtypeStruct((8, 128), f32)), *stats
    )
    part = call(join_kernel, jax.ShapeDtypeStruct((64, NC), jnp.bfloat16), *arrived, m, d)
    parts = [part, *(swap(part, k) for k in (1, 2, 3))]
    basis = call(basis_kernel, jax.ShapeDtypeStruct((K, 32 * n), f32), tc, m, d)
    image = call(spread_kernel, jax.ShapeDtypeStruct((K, 4 * NC), f32), *parts)
    return (basis.T, image.T)


def solution(mesh):
    in_specs = (P(None, ("row", "col"), None), P(None, "col", None), P("col", None))
    out_specs = (P("row", None), P("col", None))
    return jax.shard_map(body, mesh=mesh, in_specs=in_specs, out_specs=out_specs, check_vma=False)
```

profile of v0, /device:TPU:1, one launch (start us, length us, event | category | flops | bytes accessed | tf_op | source)
XLA Modules:
  0.0 116.7 jit_solution(10161409668222117080)
XLA Ops:
  0.6 3.8 %collective-permute-start = (bf16[3,32,512]{2,1,0:T(8,128)(2,1)}, bf16[3,32,512]{2,1,0:T(8,128)(2,1)S(1)}, u32[]{:S(2)}, u32[]{:S(2)}) collective-permute-start(bf16[3,32,512]{2,1,0:T(8,128)(2,1)} %mine.1), channel_id=1, source_target_pairs={{0,16},{1,17},{2,18},{3,19},{4,20},{5,21},{6,22},{7,23},{8,24},{9,... | collective-permute-start | bytes 294920 | tf_op jit(solution)/shard_map/ppermute | solution.py:479
  5.6 4.0 %columns.1 = (bf16[3,1024,512]{2,1,0:T(8,128)(2,1)S(1)}, f32[8,1024]{1,0:T(8,128)S(1)}) custom-call(bf16[3,1024,512]{2,1,0:T(8,128)(2,1)} %coords.1), custom_call_target="tpu_custom_call" | custom-call | flops 15728640 | bytes 6291456 | tf_op jit(solution)/shard_map/columns/pallas_call | solution.py:43
  9.7 1.3 %collective-permute-start.1 = (bf16[3,64,512]{2,1,0:T(8,128)(2,1)S(1)}, bf16[3,64,512]{2,1,0:T(8,128)(2,1)S(1)}, u32[]{:S(2)}, u32[]{:S(2)}) collective-permute-start(bf16[3,64,512]{2,1,0:T(8,128)(2,1)S(1)} %shard_map.50.p0), channel_id=1, source_target_pairs={{0,1},{1,2},{2,3},{3,0},{4,5},{5,6},{6,7},{7,4},{8,9},{9,10},{10,1... | collective-permute-start | bytes 589832 | tf_op jit(solution)/shard_map/ppermute | solution.py:479
  11.0 1.5 %collective-permute-start.2 = (bf16[3,64,512]{2,1,0:T(8,128)(2,1)S(1)}, bf16[3,64,512]{2,1,0:T(8,128)(2,1)S(1)}, u32[]{:S(2)}, u32[]{:S(2)}) collective-permute-start(bf16[3,64,512]{2,1,0:T(8,128)(2,1)S(1)} %shard_map.50.p0), channel_id=1, source_target_pairs={{0,3},{1,0},{2,1},{3,2},{4,7},{5,4},{6,5},{7,6},{8,11},{9,8},{10,9... | collective-permute-start | bytes 589832 | tf_op jit(solution)/shard_map/ppermute | solution.py:479
  12.4 1.5 %collective-permute-start.3 = (bf16[3,64,512]{2,1,0:T(8,128)(2,1)S(1)}, bf16[3,64,512]{2,1,0:T(8,128)(2,1)S(1)}, u32[]{:S(2)}, u32[]{:S(2)}) collective-permute-start(bf16[3,64,512]{2,1,0:T(8,128)(2,1)S(1)} %shard_map.50.p0), channel_id=1, source_target_pairs={{0,2},{1,3},{2,0},{3,1},{4,6},{5,7},{6,4},{7,5},{8,10},{9,11},{10,... | collective-permute-start | bytes 589832 | tf_op jit(solution)/shard_map/ppermute | solution.py:479
  14.0 1.5 %collective-permute-done.1.p1 = bf16[3,64,512]{2,1,0:T(8,128)(2,1)S(1)} collective-permute-done((bf16[3,64,512]{2,1,0:T(8,128)(2,1)S(1)}, bf16[3,64,512]{2,1,0:T(8,128)(2,1)S(1)}, u32[]{:S(2)}, u32[]{:S(2)}) %collective-permute-start.1) | collective-permute-done | bytes 196640 | tf_op jit(solution)/shard_map/ppermute | solution.py:479
  15.5 3.1 %collective-permute-done.3.p3 = bf16[3,64,512]{2,1,0:T(8,128)(2,1)S(1)} collective-permute-done((bf16[3,64,512]{2,1,0:T(8,128)(2,1)S(1)}, bf16[3,64,512]{2,1,0:T(8,128)(2,1)S(1)}, u32[]{:S(2)}, u32[]{:S(2)}) %collective-permute-start.3) | collective-permute-done | bytes 196640 | tf_op jit(solution)/shard_map/ppermute | solution.py:479
  19.5 3.7 %collective-permute-start.6 = (bf16[3,256,512]{2,1,0:T(8,128)(2,1)}, bf16[3,256,512]{2,1,0:T(8,128)(2,1)S(1)}, u32[]{:S(2)}, u32[]{:S(2)}) collective-permute-start(bf16[3,256,512]{2,1,0:T(8,128)(2,1)} %get-tuple-element.28), channel_id=1, source_target_pairs={{0,8},{1,9},{2,10},{3,11},{4,12},{5,13},{6,14},{7,15},{8,0},{9,1},... | collective-permute-start | bytes 2359304 | tf_op jit(solution)/shard_map/ppermute | solution.py:479
  23.3 1.1 collective-permute-start.4
  24.4 1.6 %collective-permute-start.5 = (bf16[3,256,512]{2,1,0:T(8,128)(2,1)}, bf16[3,256,512]{2,1,0:T(8,128)(2,1)S(1)}, u32[]{:S(2)}, u32[]{:S(2)}) collective-permute-start(bf16[3,256,512]{2,1,0:T(8,128)(2,1)} %get-tuple-element.28), channel_id=1, source_target_pairs={{0,12},{1,13},{2,14},{3,15},{4,0},{5,1},{6,2},{7,3},{8,4},{9,5},{1... | collective-permute-start | bytes 2359304 | tf_op jit(solution)/shard_map/ppermute | solution.py:479
  26.3 8.8 %shard_map.51 = (bf16[256,1024]{1,0:T(8,128)(2,1)}, bf16[256,1024]{1,0:T(8,128)(2,1)}, f32[256,256]{1,0:T(8,128)S(1)}) custom-call(bf16[3,256,512]{2,1,0:T(8,128)(2,1)S(1)} %get-tuple-element.24.refs_0_, bf16[3,1024,512]{2,1,0:T(8,128)(2,1)S(1)} %get-tuple-element.25.refs_1_.refs_2_, f32[8,1024]{1,0:T(8,128)S(1)} %get-tuple-element.26.refs_2_.refs_3_, ...), custom_call_target="tpu_custom_call" | custom-call | flops 2415919104 | bytes 8388608 | tf_op jit(solution)/shard_map/pallas_call | solution.py:199
  35.1 8.7 %shard_map.53 = (bf16[256,1024]{1,0:T(8,128)(2,1)}, bf16[256,1024]{1,0:T(8,128)(2,1)}, f32[256,256]{1,0:T(8,128)S(1)}) custom-call(bf16[3,256,512]{2,1,0:T(8,128)(2,1)S(1)} %collective-permute-done.6.refs_0_, bf16[3,1024,512]{2,1,0:T(8,128)(2,1)S(1)} %get-tuple-element.25.refs_1_.refs_2_, f32[8,1024]{1,0:T(8,128)S(1)} %get-tuple-element.26.refs_2_.refs_3_, ...), custom_call_target="tpu_custom_call" | custom-call | flops 2415919104 | bytes 8388608 | tf_op jit(solution)/shard_map/pallas_call | solution.py:199
  43.8 16.6 %shard_map.52 = (bf16[512,1024]{1,0:T(8,128)(2,1)}, bf16[512,1024]{1,0:T(8,128)(2,1)}, f32[512,256]{1,0:T(8,128)S(1)}) custom-call(bf16[3,256,512]{2,1,0:T(8,128)(2,1)S(1)} %collective-permute-done.4.refs_0_, bf16[3,256,512]{2,1,0:T(8,128)(2,1)S(1)} %collective-permute-done.5.refs_1_, bf16[3,1024,512]{2,1,0:T(8,128)(2,1)S(1)} %get-tuple-element.25.refs_1_.refs_2_, ...), custom_call_target="tpu_custom_call" | custom-call | flops 4831838208 | bytes 8388608 | tf_op jit(solution)/shard_map/pallas_call | solution.py:199
  60.7 14.5 %all_to_all.10.got = f32[32,24,128]{2,1,0:T(8,128)S(1)} all-to-all(f32[32,24,128]{2,1,0:T(8,128)S(1)} %shard_map.54), channel_id=1, replica_groups=mesh['row'=4,'col'=32] {'col'}, dimensions={0} | all-to-all | bytes 786432 | tf_op jit(solution)/shard_map/all_to_all | solution.py:514
  75.2 1.1 shard_map.55
  76.4 3.9 %all-to-all-start.1 = ((f32[32,24,128]{2,1,0:T(8,128)}), f32[32,24,128]{2,1,0:T(8,128)S(1)}, u32[]{:S(2)}, u32[]{:S(2)}) async-start(f32[32,24,128]{2,1,0:T(8,128)} %shard_map.55), calls=%async_computation.1 | async-start | bytes 786432 | tf_op jit(solution)/shard_map/all_to_all | solution.py:516
  80.2 9.9 %all-to-all-done.1.got = f32[32,24,128]{2,1,0:T(8,128)S(1)} async-done(((f32[32,24,128]{2,1,0:T(8,128)}), f32[32,24,128]{2,1,0:T(8,128)S(1)}, u32[]{:S(2)}, u32[]{:S(2)}) %all-to-all-start.1) | async-done | bytes 393248 | tf_op jit(solution)/shard_map/all_to_all | solution.py:516
  91.0 6.5 %collective-permute-start.7 = (f32[72,128]{1,0:T(8,128)S(1)}, f32[72,128]{1,0:T(8,128)S(1)}, u32[]{:S(2)}, u32[]{:S(2)}) collective-permute-start(f32[72,128]{1,0:T(8,128)S(1)} %get-tuple-element.32.s0), channel_id=1, source_target_pairs={{0,32},{32,0},{64,96},{96,64},{1,33},{33,1},{65,97},{97,65},{2,34}... | collective-permute-start | bytes 110600 | tf_op jit(solution)/shard_map/ppermute | solution.py:483
  97.5 3.9 %image.1 = (f32[72,256]{1,0:T(8,128)S(1)}, f32[72,256]{1,0:T(8,128)S(1)}, f32[72,256]{1,0:T(8,128)S(1)}, f32[72,256]{1,0:T(8,128)S(1)}) custom-call(s32[1]{0:T(128)} %bitcast.3.me, bf16[144,1024]{1,0:T(8,128)(2,1)S(1)} %get-tuple-element.35.left, bf16[256,1024]{1,0:T(8,128)(2,1)S(1)} %copy-done.2, bf16[256,1024]{1,0:T(8,128)(2,1)S(1)} %copy-done.3, ...), custom_call_target="tpu_custom_call" | custom-call | flops 1073741824 | bytes 5242880 | tf_op jit(solution)/shard_map/image/pallas_call | solution.py:369
  102.0 1.7 %collective-permute-start.12 = (f32[72,256]{1,0:T(8,128)S(1)}, f32[72,256]{1,0:T(8,128)S(1)}, u32[]{:S(2)}, u32[]{:S(2)}) collective-permute-start(f32[72,256]{1,0:T(8,128)S(1)} %get-tuple-element.45), channel_id=1, source_target_pairs={{0,96},{32,64},{64,32},{96,0},{1,97},{33,65},{65,33},{97,1},{2,98}... | collective-permute-start | bytes 221192 | tf_op jit(solution)/shard_map/ppermute | solution.py:483
  105.1 2.3 %collective-permute-done.8.s2 = f32[72,128]{1,0:T(8,128)S(1)} collective-permute-done((f32[72,128]{1,0:T(8,128)S(1)}, f32[72,128]{1,0:T(8,128)S(1)}, u32[]{:S(2)}, u32[]{:S(2)}) %collective-permute-start.8) | collective-permute-done | bytes 36896 | tf_op jit(solution)/shard_map/ppermute | solution.py:483
  107.3 1.5 %collective-permute-done.9.s3 = f32[72,128]{1,0:T(8,128)S(1)} collective-permute-done((f32[72,128]{1,0:T(8,128)S(1)}, f32[72,128]{1,0:T(8,128)S(1)}, u32[]{:S(2)}, u32[]{:S(2)}) %collective-permute-start.9) | collective-permute-done | bytes 36896 | tf_op jit(solution)/shard_map/ppermute | solution.py:483
  108.8 2.0 %shard_map.57 = (f32[64,128]{1,0:T(8,128)S(1)}, f32[8,128]{1,0:T(8,128)S(1)}) custom-call(f32[72,128]{1,0:T(8,128)S(1)} %get-tuple-element.32.s0, f32[72,128]{1,0:T(8,128)S(1)} %collective-permute-done.7.s1, f32[72,128]{1,0:T(8,128)S(1)} %collective-permute-done.8.s2, f32[72,128]{1,0:T(8,128)S(1)} %collective-permute-done.9.s3), custom_call_target="tpu_custom_call" | custom-call | tf_op jit(solution)/shard_map/pallas_call | solution.py:456
  113.6 1.4 %shard_map.58 = f32[64,1024]{1,0:T(8,128)} custom-call(f32[1024,64]{1,0:T(8,128)S(1)} %get-tuple-element.31.tc, f32[64,128]{1,0:T(8,128)S(1)} %get-tuple-element.33.m, f32[8,128]{1,0:T(8,128)S(1)} %get-tuple-element.34.d), custom_call_target="tpu_custom_call" | custom-call | tf_op jit(solution)/shard_map/pallas_call | solution.py:456
  (44 shorter events, 10.0 us)
Async XLA Ops:
  0.6 8.9 %copy-start.4 = (bf16[3,32,512]{2,1,0:T(8,128)(2,1)S(1)}, bf16[3,32,512]{2,1,0:T(8,128)(2,1)}, u32[]{:S(2)}) copy-start(bf16[3,32,512]{2,1,0:T(8,128)(2,1)} %mine.1) | copy-start | bytes 294916
  0.6 22.6 %copy-start.5 = (f32[1024,64]{0,1:T(8,128)S(1)}, f32[1024,64]{0,1:T(8,128)}, u32[]{:S(2)}) copy-start(f32[1024,64]{0,1:T(8,128)} %param.5) | copy-start | bytes 786436
  0.6 8.9 %collective-permute-start = (bf16[3,32,512]{2,1,0:T(8,128)(2,1)}, bf16[3,32,512]{2,1,0:T(8,128)(2,1)S(1)}, u32[]{:S(2)}, u32[]{:S(2)}) collective-permute-start(bf16[3,32,512]{2,1,0:T(8,128)(2,1)} %mine.1), channel_id=1, source_target_pairs={{0,16},{1,17},{2,18},{3,19},{4,20},{5,21},{6,22},{7,23},{8,24},{9,... | collective-permute-start | bytes 294920 | tf_op jit(solution)/shard_map/ppermute | solution.py:479
  9.7 5.8 %collective-permute-start.1 = (bf16[3,64,512]{2,1,0:T(8,128)(2,1)S(1)}, bf16[3,64,512]{2,1,0:T(8,128)(2,1)S(1)}, u32[]{:S(2)}, u32[]{:S(2)}) collective-permute-start(bf16[3,64,512]{2,1,0:T(8,128)(2,1)S(1)} %shard_map.50.p0), channel_id=1, source_target_pairs={{0,1},{1,2},{2,3},{3,0},{4,5},{5,6},{6,7},{7,4},{8,9},{9,10},{10,1... | collective-permute-start | bytes 589832 | tf_op jit(solution)/shard_map/ppermute | solution.py:479
  11.0 4.5 %collective-permute-start.2 = (bf16[3,64,512]{2,1,0:T(8,128)(2,1)S(1)}, bf16[3,64,512]{2,1,0:T(8,128)(2,1)S(1)}, u32[]{:S(2)}, u32[]{:S(2)}) collective-permute-start(bf16[3,64,512]{2,1,0:T(8,128)(2,1)S(1)} %shard_map.50.p0), channel_id=1, source_target_pairs={{0,3},{1,0},{2,1},{3,2},{4,7},{5,4},{6,5},{7,6},{8,11},{9,8},{10,9... | collective-permute-start | bytes 589832 | tf_op jit(solution)/shard_map/ppermute | solution.py:479
  12.4 6.1 %collective-permute-start.3 = (bf16[3,64,512]{2,1,0:T(8,128)(2,1)S(1)}, bf16[3,64,512]{2,1,0:T(8,128)(2,1)S(1)}, u32[]{:S(2)}, u32[]{:S(2)}) collective-permute-start(bf16[3,64,512]{2,1,0:T(8,128)(2,1)S(1)} %shard_map.50.p0), channel_id=1, source_target_pairs={{0,2},{1,3},{2,0},{3,1},{4,6},{5,7},{6,4},{7,5},{8,10},{9,11},{10,... | collective-permute-start | bytes 589832 | tf_op jit(solution)/shard_map/ppermute | solution.py:479
  19.5 15.5 %collective-permute-start.6 = (bf16[3,256,512]{2,1,0:T(8,128)(2,1)}, bf16[3,256,512]{2,1,0:T(8,128)(2,1)S(1)}, u32[]{:S(2)}, u32[]{:S(2)}) collective-permute-start(bf16[3,256,512]{2,1,0:T(8,128)(2,1)} %get-tuple-element.28), channel_id=1, source_target_pairs={{0,8},{1,9},{2,10},{3,11},{4,12},{5,13},{6,14},{7,15},{8,0},{9,1},... | collective-permute-start | bytes 2359304 | tf_op jit(solution)/shard_map/ppermute | solution.py:479
  23.3 20.5 %collective-permute-start.4 = (bf16[3,256,512]{2,1,0:T(8,128)(2,1)}, bf16[3,256,512]{2,1,0:T(8,128)(2,1)S(1)}, u32[]{:S(2)}, u32[]{:S(2)}) collective-permute-start(bf16[3,256,512]{2,1,0:T(8,128)(2,1)} %get-tuple-element.28), channel_id=1, source_target_pairs={{0,4},{1,5},{2,6},{3,7},{4,8},{5,9},{6,10},{7,11},{8,12},{9,13},{1... | collective-permute-start | bytes 2359304 | tf_op jit(solution)/shard_map/ppermute | solution.py:479
  24.4 19.4 %collective-permute-start.5 = (bf16[3,256,512]{2,1,0:T(8,128)(2,1)}, bf16[3,256,512]{2,1,0:T(8,128)(2,1)S(1)}, u32[]{:S(2)}, u32[]{:S(2)}) collective-permute-start(bf16[3,256,512]{2,1,0:T(8,128)(2,1)} %get-tuple-element.28), channel_id=1, source_target_pairs={{0,12},{1,13},{2,14},{3,15},{4,0},{5,1},{6,2},{7,3},{8,4},{9,5},{1... | collective-permute-start | bytes 2359304 | tf_op jit(solution)/shard_map/ppermute | solution.py:479
  60.5 37.0 %copy-start = (bf16[512,1024]{1,0:T(8,128)(2,1)S(1)}, bf16[512,1024]{1,0:T(8,128)(2,1)}, u32[]{:S(2)}) copy-start(bf16[512,1024]{1,0:T(8,128)(2,1)} %get-tuple-element.38.h1) | copy-start | bytes 3145732
  60.5 37.0 %copy-start.1 = (bf16[512,1024]{1,0:T(8,128)(2,1)S(1)}, bf16[512,1024]{1,0:T(8,128)(2,1)}, u32[]{:S(2)}) copy-start(bf16[512,1024]{1,0:T(8,128)(2,1)} %get-tuple-element.39.l1) | copy-start | bytes 3145732
  60.5 37.0 %copy-start.2 = (bf16[256,1024]{1,0:T(8,128)(2,1)S(1)}, bf16[256,1024]{1,0:T(8,128)(2,1)}, u32[]{:S(2)}) copy-start(bf16[256,1024]{1,0:T(8,128)(2,1)} %get-tuple-element.36.h0) | copy-start | bytes 1572868
  60.5 37.0 %copy-start.3 = (bf16[256,1024]{1,0:T(8,128)(2,1)S(1)}, bf16[256,1024]{1,0:T(8,128)(2,1)}, u32[]{:S(2)}) copy-start(bf16[256,1024]{1,0:T(8,128)(2,1)} %get-tuple-element.37.l0) | copy-start | bytes 1572868
  76.4 13.8 %all-to-all-start.1 = ((f32[32,24,128]{2,1,0:T(8,128)}), f32[32,24,128]{2,1,0:T(8,128)S(1)}, u32[]{:S(2)}, u32[]{:S(2)}) async-start(f32[32,24,128]{2,1,0:T(8,128)} %shard_map.55), calls=%async_computation.1 | async-start | bytes 786432 | tf_op jit(solution)/shard_map/all_to_all | solution.py:516
  91.0 13.0 %collective-permute-start.7 = (f32[72,128]{1,0:T(8,128)S(1)}, f32[72,128]{1,0:T(8,128)S(1)}, u32[]{:S(2)}, u32[]{:S(2)}) collective-permute-start(f32[72,128]{1,0:T(8,128)S(1)} %get-tuple-element.32.s0), channel_id=1, source_target_pairs={{0,32},{32,0},{64,96},{96,64},{1,33},{33,1},{65,97},{97,65},{2,34}... | collective-permute-start | bytes 110600 | tf_op jit(solution)/shard_map/ppermute | solution.py:483
  101.4 9.4 %collective-permute-start.10 = (f32[72,256]{1,0:T(8,128)S(1)}, f32[72,256]{1,0:T(8,128)S(1)}, u32[]{:S(2)}, u32[]{:S(2)}) collective-permute-start(f32[72,256]{1,0:T(8,128)S(1)} %get-tuple-element.43), channel_id=1, source_target_pairs={{0,32},{32,0},{64,96},{96,64},{1,33},{33,1},{65,97},{97,65},{2,34}... | collective-permute-start | bytes 221192 | tf_op jit(solution)/shard_map/ppermute | solution.py:483
  101.5 9.3 %collective-permute-start.11 = (f32[72,256]{1,0:T(8,128)S(1)}, f32[72,256]{1,0:T(8,128)S(1)}, u32[]{:S(2)}, u32[]{:S(2)}) collective-permute-start(f32[72,256]{1,0:T(8,128)S(1)} %get-tuple-element.44), channel_id=1, source_target_pairs={{0,64},{32,96},{64,0},{96,32},{1,65},{33,97},{65,1},{97,33},{2,66}... | collective-permute-start | bytes 221192 | tf_op jit(solution)/shard_map/ppermute | solution.py:483
  102.0 8.9 %collective-permute-start.12 = (f32[72,256]{1,0:T(8,128)S(1)}, f32[72,256]{1,0:T(8,128)S(1)}, u32[]{:S(2)}, u32[]{:S(2)}) collective-permute-start(f32[72,256]{1,0:T(8,128)S(1)} %get-tuple-element.45), channel_id=1, source_target_pairs={{0,96},{32,64},{64,32},{96,0},{1,97},{33,65},{65,33},{97,1},{2,98}... | collective-permute-start | bytes 221192 | tf_op jit(solution)/shard_map/ppermute | solution.py:483
  103.6 3.7 %collective-permute-start.8 = (f32[72,128]{1,0:T(8,128)S(1)}, f32[72,128]{1,0:T(8,128)S(1)}, u32[]{:S(2)}, u32[]{:S(2)}) collective-permute-start(f32[72,128]{1,0:T(8,128)S(1)} %get-tuple-element.32.s0), channel_id=1, source_target_pairs={{0,64},{32,96},{64,0},{96,32},{1,65},{33,97},{65,1},{97,33},{2,66}... | collective-permute-start | bytes 110600 | tf_op jit(solution)/shard_map/ppermute | solution.py:483
  104.0 4.8 %collective-permute-start.9 = (f32[72,128]{1,0:T(8,128)S(1)}, f32[72,128]{1,0:T(8,128)S(1)}, u32[]{:S(2)}, u32[]{:S(2)}) collective-permute-start(f32[72,128]{1,0:T(8,128)S(1)} %get-tuple-element.32.s0), channel_id=1, source_target_pairs={{0,96},{32,64},{64,32},{96,0},{1,97},{33,65},{65,33},{97,1},{2,98}... | collective-permute-start | bytes 110600 | tf_op jit(solution)/shard_map/ppermute | solution.py:483
  111.4 3.6 %collective-permute-start.13 = (bf16[64,256]{1,0:T(8,128)(2,1)S(1)}, bf16[64,256]{1,0:T(8,128)(2,1)S(1)}, u32[]{:S(2)}, u32[]{:S(2)}) collective-permute-start(bf16[64,256]{1,0:T(8,128)(2,1)S(1)} %shard_map.59.i0), channel_id=1, source_target_pairs={{0,32},{32,0},{64,96},{96,64},{1,33},{33,1},{65,97},{97,65},{2,34}... | collective-permute-start | bytes 98312 | tf_op jit(solution)/shard_map/ppermute | solution.py:483
  111.8 3.3 %collective-permute-start.14 = (bf16[64,256]{1,0:T(8,128)(2,1)S(1)}, bf16[64,256]{1,0:T(8,128)(2,1)S(1)}, u32[]{:S(2)}, u32[]{:S(2)}) collective-permute-start(bf16[64,256]{1,0:T(8,128)(2,1)S(1)} %shard_map.59.i0), channel_id=1, source_target_pairs={{0,64},{32,96},{64,0},{96,32},{1,65},{33,97},{65,1},{97,33},{2,66}... | collective-permute-start | bytes 98312 | tf_op jit(solution)/shard_map/ppermute | solution.py:483
  112.5 3.4 %collective-permute-start.15 = (bf16[64,256]{1,0:T(8,128)(2,1)S(1)}, bf16[64,256]{1,0:T(8,128)(2,1)S(1)}, u32[]{:S(2)}, u32[]{:S(2)}) collective-permute-start(bf16[64,256]{1,0:T(8,128)(2,1)S(1)} %shard_map.59.i0), channel_id=1, source_target_pairs={{0,96},{32,64},{64,32},{96,0},{1,97},{33,65},{65,33},{97,1},{2,98}... | collective-permute-start | bytes 98312 | tf_op jit(solution)/shard_map/ppermute | solution.py:483
where the time goes:
time: 117 us
  Pallas kernels  49.9 us (43%)
  starting transfers between devices  30.8 us (26%)
  waiting for transfers between devices  19.2 us (16%)
  blocking collectives  14.5 us (12%)
  other arithmetic  1.37 us (1%)
    pallas_call x3, Pallas kernels, dist_call(): pl.pallas_call(functools.partial(dist_kernel, len(sources)), grid=(nc //...  34.1 us
    ppermute x7, starting transfers between devices, shift(): return lax.ppermute(a, ('row', 'col'), pairs)  14.5 us
    all_to_all x1, blocking collectives, body(): got = lax.all_to_all(sent, 'col', 0, 0, tiled=True)  14.5 us
    ppermute x9, starting transfers between devices, swap(): return lax.ppermute(a, 'row', [(r, r ^ k) for r in range(4)])  12.4 us
    all_to_all x1, waiting for transfers between devices, body(): got = lax.all_to_all(totals, 'col', 0, 0, tiled=True)  9.93 us
    pallas_call x8, Pallas kernels, call(): pl.pallas_call(kernel, out_shape=outs, in_specs=[pl.BlockSpec(memory_spac...  6.96 us
    ppermute x9, waiting for transfers between devices, swap(): return lax.ppermute(a, 'row', [(r, r ^ k) for r in range(4)])  4.67 us
    ppermute x7, waiting for transfers between devices, shift(): return lax.ppermute(a, ('row', 'col'), pairs)  4.62 us
  transfers between devices with their start and end apart: 17, of which 6 were waited for; matrix products, arithmetic and copies ran while one was open for 1% of the time, Pallas kernels for 25%

commit v1 on v0

--- a/solution.py
+++ b/solution.py
@@ -13,6 +13,9 @@
 K = 64
 TR = 128
 TC = 512
+SR, SC = 16, 512
+UNIT_AT = (0, 1, 2, 3, 4, 5)
+PANEL_AT = 6
 NC = 256
 RF = 4096
 CF = 32768
@@ -108,7 +111,7 @@
     rows = refs[:ns]
     cols, cn, sw = refs[ns : ns + 3]
     outs, t_out = refs[ns + 3 : ns + 5], refs[ns + 5]
-    bufs, rn, kept, sems = refs[ns + 6 : ns + 8], refs[ns + 8], refs[ns + 9 : ns + 11], refs[ns + 11]
+    bufs, rn, kept, sems = refs[ns + 6 : ns + 8], refs[ns + 8], refs[ns + 9], refs[ns + 10]
     nb = rn.shape[0]
     per = nb // ns
     ct = pl.program_id(0)
@@ -128,33 +131,30 @@
 
     def newton(rb, buf, slices):
         for r, c in slices:
-            p = [[buf[b, a * TR + r : a * TR + r + 16, c : c + 128] for b in range(3)] for a in range(3)]
-            u = rn[rb, r : r + 16] + cn[0:1, c : c + 128]
+            p = [[buf[b, a * TR + r : a * TR + r + SR, c : c + SC] for b in range(3)] for a in range(3)]
+            u = rn[rb, r : r + SR, 0:SC] + cn[0:1, c : c + SC]
             d = newton_slice(p, u)
             h = d.astype(jnp.bfloat16)
-            kept[0][ct, rb * TR + r : rb * TR + r + 16, c : c + 128] = h
-            kept[1][ct, rb * TR + r : rb * TR + r + 16, c : c + 128] = (d - h.astype(jnp.float32)).astype(jnp.bfloat16)
+            kept[ct, rb, 0, r : r + SR, c : c + SC] = h
+            kept[ct, rb, 1, r : r + SR, c : c + SC] = (d - h.astype(jnp.float32)).astype(jnp.bfloat16)
 
     def stores(at, rb):
         rows_at = pl.ds(rb * TR, TR)
         return [
             pltpu.make_async_copy(
-                kept[i].at[at, rows_at, :], outs[i].at[rows_at, pl.ds(pl.multiple_of(at * TC, TC), TC)], sems.at[i, at, rb]
+                kept.at[at, rb, i], outs[i].at[rows_at, pl.ds(pl.multiple_of(at * TC, TC), TC)], sems.at[i, at, rb]
             )
             for i in range(2)
         ]
 
     def panel(rb):
-        at = slice(rb * TR, rb * TR + TR)
         w = sw[:, pl.ds(pl.multiple_of(ct * TC, TC), TC)]
-        dims = (((1,), (1,)), ((), ()))
-        t_out[at, :] += lax.dot_general(
-            kept[0][ct, at, :], w, dims, preferred_element_type=jnp.float32
-        ) + lax.dot_general(kept[1][ct, at, :], w, dims, preferred_element_type=jnp.float32)
+        both = kept[ct, rb].reshape(2 * TR, TC)
+        t = lax.dot_general(both, w, (((1,), (1,)), ((), ())), preferred_element_type=jnp.float32)
+        t_out[rb * TR : rb * TR + TR, :] += t[0:TR] + t[TR : 2 * TR]
 
     units = [(b, n) for n in range(TC // 256) for b in range(3)]
-    slices = [(r, c) for r in range(0, TR, 16) for c in range(0, TC, 128)]
-    share = -(-len(slices) // len(units))
+    slices = [(r, c) for r in range(0, TR, SR) for c in range(0, TC, SC)]
 
     @pl.when(ct == 0)
     def _():
@@ -162,7 +162,7 @@
         for rb in range(nb):
             w = frames(rb).astype(jnp.float32)
             n = jnp.sum(jnp.sum(w * w, axis=0), axis=1, keepdims=True) * (2.0 * ATOMS / 16.0)
-            rn[rb] = jnp.broadcast_to(n, (TR, 128))
+            rn[rb] = jnp.broadcast_to(n, (TR, SC))
         products(0, 0, bufs[0], units)
 
     for rb in range(nb):
@@ -170,11 +170,13 @@
 
         @pl.when(ct <= last)
         def _(rb=rb, after=after, at=at):
-            for i in range(len(units)):
-                newton(rb, bufs[rb % 2], slices[i * share : (i + 1) * share])
-                products(after, at, bufs[(rb + 1) % 2], units[i : i + 1])
-                if i == 2 and rb > 0:
+            for i in range(len(slices)):
+                if i in UNIT_AT:
+                    j = UNIT_AT.index(i)
+                    products(after, at, bufs[(rb + 1) % 2], units[j : j + 1])
+                if i == PANEL_AT and rb > 0:
                     panel(rb - 1)
+                newton(rb, bufs[rb % 2], slices[i : i + 1])
 
         for copy in stores(ct, rb):
             copy.start()
@@ -214,9 +216,8 @@
         scratch_shapes=[
             pltpu.VMEM((3, 3 * TR, TC), jnp.float32),
             pltpu.VMEM((3, 3 * TR, TC), jnp.float32),
-            pltpu.VMEM((r // TR, TR, 128), jnp.float32),
-            pltpu.VMEM((nc // TC, r, TC), jnp.bfloat16),
-            pltpu.VMEM((nc // TC, r, TC), jnp.bfloat16),
+            pltpu.VMEM((r // TR, TR, SC), jnp.float32),
+            pltpu.VMEM((nc // TC, r // TR, 2, TR, TC), jnp.bfloat16),
             pltpu.SemaphoreType.DMA((2, nc // TC, r // TR)),
         ],
         compiler_params=pltpu.CompilerParams(dimension_semantics=("arbitrary",), vmem_limit_bytes=20 << 20),
@@ -330,56 +331,50 @@
     left[128:144, :] = jnp.ones((16, pt.shape[1]), jnp.bfloat16)
 
 
-def image_kernel(me, left, h0, l0, h1, l1, h2, l2, *refs):
-    outs, late, sems = refs[:4], refs[4], refs[5]
-    k = pl.program_id(0)
+def image_kernel(left, h0, l0, h1, l1, h2, l2, o0, o1, o2, o3, late, acc, sems):
     copies = [pltpu.make_async_copy(ref, late.at[i], sems.at[i]) for i, ref in enumerate((h2, l2))]
-
-    @pl.when(k == 0)
-    def _():
-        for copy in copies:
-            copy.start()
-
-    acc = jnp.zeros((144, NC), jnp.float32)
-    for at, refs in zip(CHUNK_START, ((h0, l0), (h1, l1))):
-        for ref in refs:
-            acc += jnp.dot(left[:, at : at + ref.shape[0]], ref[...], preferred_element_type=jnp.float32)
-
-    @pl.when(k == 0)
-    def _():
-        for copy in copies:
-            copy.wait()
-
-    mine = pl.ds(pl.multiple_of((me[0] ^ k) * NC, NC), NC)
-    for i in range(2):
-        acc += jnp.dot(left[:, CHUNK_START[2] :], late[i, :, mine], preferred_element_type=jnp.float32)
-    for j in range(4):
-
-        @pl.when(k == j)
-        def _(j=j):
-            outs[j][0:64, :] = acc[0:64] + acc[64:128]
-            outs[j][64:72, :] = acc[128:136]
-
-
-def image_call(me, left, chunks):
+    for copy in copies:
+        copy.start()
+
+    def block(k):
+        return pl.ds(pl.multiple_of((lax.axis_index("row") ^ k) * NC, NC), NC)
+
+    for k in range(4):
+        total = jnp.zeros((144, NC), jnp.float32)
+        for at, refs in zip(CHUNK_START, ((h0, l0), (h1, l1))):
+            for ref in refs:
+                total += jnp.dot(
+                    left[:, at : at + ref.shape[0]], ref[:, block(k)], preferred_element_type=jnp.float32
+                )
+        acc[k] = total
+    for copy in copies:
+        copy.wait()
+    for k, out in enumerate((o0, o1, o2, o3)):
+        total = acc[k]
+        for i in range(2):
+            total += jnp.dot(left[:, CHUNK_START[2] :], late[i, :, block(k)], preferred_element_type=jnp.float32)
+        out[0:64, :] = total[0:64] + total[64:128]
+        out[64:72, :] = total[128:136]
+
+
+def image_call(left, chunks):
     flat = [a for c in chunks for a in c[:2]]
     flat[4:] = [pltpu.with_memory_space_constraint(a, pltpu.HBM) for a in flat[4:]]
-    spec = lambda a: pl.BlockSpec((a.shape[0], NC), lambda k, me: (0, me[0] ^ k))
-    hbm = pl.BlockSpec(memory_space=pltpu.HBM)
+    vmem = pl.BlockSpec(memory_space=pltpu.VMEM)
     return pl.pallas_call(
         image_kernel,
-        grid_spec=pltpu.PrefetchScalarGridSpec(
-            num_scalar_prefetch=1,
-            grid=(4,),
-            in_specs=[pl.BlockSpec(left.shape, lambda k, me: (0, 0))] + [spec(a) for a in flat[:4]] + [hbm] * 2,
-            out_specs=[pl.BlockSpec((72, NC), lambda k, me: (0, 0))] * 4,
-            scratch_shapes=[pltpu.VMEM((2, *flat[4].shape), jnp.bfloat16), pltpu.SemaphoreType.DMA((2,))],
-        ),
+        in_specs=[vmem] * 5 + [pl.BlockSpec(memory_space=pltpu.HBM)] * 2,
+        out_specs=[vmem] * 4,
+        scratch_shapes=[
+            pltpu.VMEM((2, *flat[4].shape), jnp.bfloat16),
+            pltpu.VMEM((4, 144, NC), jnp.float32),
+            pltpu.SemaphoreType.DMA((2,)),
+        ],
         out_shape=[jax.ShapeDtypeStruct((72, NC), jnp.float32)] * 4,
-        compiler_params=pltpu.CompilerParams(dimension_semantics=("arbitrary",), vmem_limit_bytes=16 << 20),
+        compiler_params=pltpu.CompilerParams(vmem_limit_bytes=12 << 20),
         cost_estimate=pl.CostEstimate(flops=2 * 2 * 256 * 1024 * 1024, bytes_accessed=5 << 20, transcendentals=0),
         name="image",
-    )(me, left, *flat)
+    )(left, *flat)
 
 
 def factor_kernel(s0, s1, s2, s3, m_out, d_out):
@@ -483,6 +478,11 @@
     return lax.ppermute(a, "row", [(r, r ^ k) for r in range(4)])
 
 
+def exchanged(arrays):
+    got = {k: swap(arrays[k], k) for k in (3, 2, 1)}
+    return [got[k] for k in (1, 2, 3)]
+
+
 def from_three(a, axis):
     return [shift(a, **{axis: -o}) for o in OFFSETS[1:]]
 
@@ -524,17 +524,16 @@
         got,
         scratch=[pltpu.VMEM((32 * n, 128), f32)],
     )
-    me = lax.axis_index("row").reshape(1)
-    stats = [stat]
-    for k in (1, 2, 3):
-        stats.append(swap(stat, k))
-    partial = image_call(me, left, chunks)
-    arrived = [partial[0], *(swap(partial[k], k) for k in (1, 2, 3))]
+    stats = [stat, None, None, None]
+    for k in (3, 2, 1):
+        stats[k] = swap(stat, k)
+    partial = image_call(left, chunks)
+    arrived = [partial[0], *exchanged(partial)]
     m, d = call(
         factor_kernel, (jax.ShapeDtypeStruct((64, 128), f32), jax.ShapeDtypeStruct((8, 128), f32)), *stats
     )
     part = call(join_kernel, jax.ShapeDtypeStruct((64, NC), jnp.bfloat16), *arrived, m, d)
-    parts = [part, *(swap(part, k) for k in (1, 2, 3))]
+    parts = [part, *exchanged([part] * 4)]
     basis = call(basis_kernel, jax.ShapeDtypeStruct((K, 32 * n), f32), tc, m, d)
     image = call(spread_kernel, jax.ShapeDtypeStruct((K, 4 * NC), f32), *parts)
     return (basis.T, image.T)

time: 117 us -> 111 us (0.949)
  blocking collectives: 14.5 us -> 28.8 us
  waiting for transfers between devices: 19.2 us -> 9.4 us
  Pallas kernels: 49.9 us -> 43.8 us
  starting transfers between devices: 30.8 us -> 26.9 us
    all_to_all x0 -> x1, blocking collectives: none -> 13.6 us  [body(): got = lax.all_to_all(totals, 'col', 0, 0, tiled=True)]
    all_to_all x1 -> x0, waiting for transfers between devices: 9.93 us -> none  [body(): got = lax.all_to_all(totals, 'col', 0, 0, tiled=True)]
    all_to_all x1 -> x0, starting transfers between devices: 3.88 us -> none  [body(): got = lax.all_to_all(totals, 'col', 0, 0, tiled=True)]
    pallas_call x3, Pallas kernels: 34.1 us -> 30.7 us  [dist_call(): pl.pallas_call(functools.partial(dist_kernel, len(sources)), grid=(nc //...]
    pallas_call x1, Pallas kernels: 3.89 us -> 1.95 us  [image_call(): pl.pallas_call(image_kernel, in_specs=[vmem] * 5 + [pl.BlockSpec(memory_s...]
  transfers between devices with their start and end apart: 17 -> 16, of which waited for: 6 -> 6; matrix products, arithmetic and copies ran while one was open for 1% -> 1% of each run, Pallas kernels for 25% -> 23%
where the time goes in v1:
time: 111 us
  Pallas kernels  43.8 us (39%)
  blocking collectives  28.8 us (26%)
  starting transfers between devices  26.9 us (24%)
  waiting for transfers between devices  9.4 us (8%)
  other arithmetic  1.37 us (1%)
    pallas_call x3, Pallas kernels, dist_call(): pl.pallas_call(functools.partial(dist_kernel, len(sources)), grid=(nc //...  30.7 us
    all_to_all x1, blocking collectives, body(): got = lax.all_to_all(sent, 'col', 0, 0, tiled=True)  15.2 us
    ppermute x7, starting transfers between devices, shift(): return lax.ppermute(a, ('row', 'col'), pairs)  14.5 us
    all_to_all x1, blocking collectives, body(): got = lax.all_to_all(totals, 'col', 0, 0, tiled=True)  13.6 us
    ppermute x9, starting transfers between devices, swap(): return lax.ppermute(a, 'row', [(r, r ^ k) for r in range(4)])  12.4 us
    pallas_call x8, Pallas kernels, call(): pl.pallas_call(kernel, out_shape=outs, in_specs=[pl.BlockSpec(memory_spac...  6.19 us
    ppermute x7, waiting for transfers between devices, shift(): return lax.ppermute(a, ('row', 'col'), pairs)  4.74 us
    ppermute x9, waiting for transfers between devices, swap(): return lax.ppermute(a, 'row', [(r, r ^ k) for r in range(4)])  4.67 us
  transfers between devices with their start and end apart: 16, of which 6 were waited for; matrix products, arithmetic and copies ran while one was open for 1% of the time, Pallas kernels for 23%

profile of v1, /device:TPU:1, one launch (start us, length us, event | category | flops | bytes accessed | tf_op | source)
XLA Modules:
  0.0 111.2 jit_solution(11592546724164481735)
XLA Ops:
  0.6 3.8 %collective-permute-start = (bf16[3,32,512]{2,1,0:T(8,128)(2,1)}, bf16[3,32,512]{2,1,0:T(8,128)(2,1)S(1)}, u32[]{:S(2)}, u32[]{:S(2)}) collective-permute-start(bf16[3,32,512]{2,1,0:T(8,128)(2,1)} %mine.1), channel_id=1, source_target_pairs={{0,16},{1,17},{2,18},{3,19},{4,20},{5,21},{6,22},{7,23},{8,24},{9,... | collective-permute-start | bytes 294920 | tf_op jit(solution)/shard_map/ppermute | solution.py:474
  4.5 1.1 reduce_sum.9
  5.6 4.0 %columns.1 = (bf16[3,1024,512]{2,1,0:T(8,128)(2,1)S(1)}, f32[8,1024]{1,0:T(8,128)S(1)}) custom-call(bf16[3,1024,512]{2,1,0:T(8,128)(2,1)} %coords.1), custom_call_target="tpu_custom_call" | custom-call | flops 15728640 | bytes 6291456 | tf_op jit(solution)/shard_map/columns/pallas_call | solution.py:46
  9.7 1.3 %collective-permute-start.1 = (bf16[3,64,512]{2,1,0:T(8,128)(2,1)S(1)}, bf16[3,64,512]{2,1,0:T(8,128)(2,1)S(1)}, u32[]{:S(2)}, u32[]{:S(2)}) collective-permute-start(bf16[3,64,512]{2,1,0:T(8,128)(2,1)S(1)} %shard_map.50.p0), channel_id=1, source_target_pairs={{0,1},{1,2},{2,3},{3,0},{4,5},{5,6},{6,7},{7,4},{8,9},{9,10},{10,1... | collective-permute-start | bytes 589832 | tf_op jit(solution)/shard_map/ppermute | solution.py:474
  11.0 1.5 %collective-permute-start.2 = (bf16[3,64,512]{2,1,0:T(8,128)(2,1)S(1)}, bf16[3,64,512]{2,1,0:T(8,128)(2,1)S(1)}, u32[]{:S(2)}, u32[]{:S(2)}) collective-permute-start(bf16[3,64,512]{2,1,0:T(8,128)(2,1)S(1)} %shard_map.50.p0), channel_id=1, source_target_pairs={{0,3},{1,0},{2,1},{3,2},{4,7},{5,4},{6,5},{7,6},{8,11},{9,8},{10,9... | collective-permute-start | bytes 589832 | tf_op jit(solution)/shard_map/ppermute | solution.py:474
  12.4 1.5 %collective-permute-start.3 = (bf16[3,64,512]{2,1,0:T(8,128)(2,1)S(1)}, bf16[3,64,512]{2,1,0:T(8,128)(2,1)S(1)}, u32[]{:S(2)}, u32[]{:S(2)}) collective-permute-start(bf16[3,64,512]{2,1,0:T(8,128)(2,1)S(1)} %shard_map.50.p0), channel_id=1, source_target_pairs={{0,2},{1,3},{2,0},{3,1},{4,6},{5,7},{6,4},{7,5},{8,10},{9,11},{10,... | collective-permute-start | bytes 589832 | tf_op jit(solution)/shard_map/ppermute | solution.py:474
  14.0 1.5 %collective-permute-done.1.p1 = bf16[3,64,512]{2,1,0:T(8,128)(2,1)S(1)} collective-permute-done((bf16[3,64,512]{2,1,0:T(8,128)(2,1)S(1)}, bf16[3,64,512]{2,1,0:T(8,128)(2,1)S(1)}, u32[]{:S(2)}, u32[]{:S(2)}) %collective-permute-start.1) | collective-permute-done | bytes 196640 | tf_op jit(solution)/shard_map/ppermute | solution.py:474
  15.5 3.1 %collective-permute-done.3.p3 = bf16[3,64,512]{2,1,0:T(8,128)(2,1)S(1)} collective-permute-done((bf16[3,64,512]{2,1,0:T(8,128)(2,1)S(1)}, bf16[3,64,512]{2,1,0:T(8,128)(2,1)S(1)}, u32[]{:S(2)}, u32[]{:S(2)}) %collective-permute-start.3) | collective-permute-done | bytes 196640 | tf_op jit(solution)/shard_map/ppermute | solution.py:474
  19.5 3.7 %collective-permute-start.6 = (bf16[3,256,512]{2,1,0:T(8,128)(2,1)}, bf16[3,256,512]{2,1,0:T(8,128)(2,1)S(1)}, u32[]{:S(2)}, u32[]{:S(2)}) collective-permute-start(bf16[3,256,512]{2,1,0:T(8,128)(2,1)} %get-tuple-element.28), channel_id=1, source_target_pairs={{0,8},{1,9},{2,10},{3,11},{4,12},{5,13},{6,14},{7,15},{8,0},{9,1},... | collective-permute-start | bytes 2359304 | tf_op jit(solution)/shard_map/ppermute | solution.py:474
  23.3 1.1 collective-permute-start.4
  24.4 1.6 %collective-permute-start.5 = (bf16[3,256,512]{2,1,0:T(8,128)(2,1)}, bf16[3,256,512]{2,1,0:T(8,128)(2,1)S(1)}, u32[]{:S(2)}, u32[]{:S(2)}) collective-permute-start(bf16[3,256,512]{2,1,0:T(8,128)(2,1)} %get-tuple-element.28), channel_id=1, source_target_pairs={{0,12},{1,13},{2,14},{3,15},{4,0},{5,1},{6,2},{7,3},{8,4},{9,5},{1... | collective-permute-start | bytes 2359304 | tf_op jit(solution)/shard_map/ppermute | solution.py:474
  26.3 8.1 %shard_map.51 = (bf16[256,1024]{1,0:T(8,128)(2,1)}, bf16[256,1024]{1,0:T(8,128)(2,1)}, f32[256,256]{1,0:T(8,128)S(1)}) custom-call(bf16[3,256,512]{2,1,0:T(8,128)(2,1)S(1)} %get-tuple-element.24.refs_0_, bf16[3,1024,512]{2,1,0:T(8,128)(2,1)S(1)} %get-tuple-element.25.refs_1_.refs_2_, f32[8,1024]{1,0:T(8,128)S(1)} %get-tuple-element.26.refs_2_.refs_3_, ...), custom_call_target="tpu_custom_call" | custom-call | flops 2415919104 | bytes 8388608 | tf_op jit(solution)/shard_map/pallas_call | solution.py:201
  34.4 8.1 %shard_map.53 = (bf16[256,1024]{1,0:T(8,128)(2,1)}, bf16[256,1024]{1,0:T(8,128)(2,1)}, f32[256,256]{1,0:T(8,128)S(1)}) custom-call(bf16[3,256,512]{2,1,0:T(8,128)(2,1)S(1)} %collective-permute-done.6.refs_0_, bf16[3,1024,512]{2,1,0:T(8,128)(2,1)S(1)} %get-tuple-element.25.refs_1_.refs_2_, f32[8,1024]{1,0:T(8,128)S(1)} %get-tuple-element.26.refs_2_.refs_3_, ...), custom_call_target="tpu_custom_call" | custom-call | flops 2415919104 | bytes 8388608 | tf_op jit(solution)/shard_map/pallas_call | solution.py:201
  42.6 14.6 %shard_map.52 = (bf16[512,1024]{1,0:T(8,128)(2,1)}, bf16[512,1024]{1,0:T(8,128)(2,1)}, f32[512,256]{1,0:T(8,128)S(1)}) custom-call(bf16[3,256,512]{2,1,0:T(8,128)(2,1)S(1)} %collective-permute-done.4.refs_0_, bf16[3,256,512]{2,1,0:T(8,128)(2,1)S(1)} %collective-permute-done.5.refs_1_, bf16[3,1024,512]{2,1,0:T(8,128)(2,1)S(1)} %get-tuple-element.25.refs_1_.refs_2_, ...), custom_call_target="tpu_custom_call" | custom-call | flops 4831838208 | bytes 8388608 | tf_op jit(solution)/shard_map/pallas_call | solution.py:201
  57.4 15.2 %all_to_all.10.got = f32[32,24,128]{2,1,0:T(8,128)S(1)} all-to-all(f32[32,24,128]{2,1,0:T(8,128)S(1)} %shard_map.54), channel_id=1, replica_groups=mesh['row'=4,'col'=32] {'col'}, dimensions={0} | all-to-all | bytes 786432 | tf_op jit(solution)/shard_map/all_to_all | solution.py:514
  73.0 13.6 %all_to_all.11.got = f32[32,24,128]{2,1,0:T(8,128)S(1)} all-to-all(f32[32,24,128]{2,1,0:T(8,128)S(1)} %shard_map.55), channel_id=1, replica_groups=mesh['row'=4,'col'=32] {'col'}, dimensions={0} | all-to-all | bytes 786432 | tf_op jit(solution)/shard_map/all_to_all | solution.py:516
  87.4 6.5 %collective-permute-start.7 = (f32[72,128]{1,0:T(8,128)S(1)}, f32[72,128]{1,0:T(8,128)S(1)}, u32[]{:S(2)}, u32[]{:S(2)}) collective-permute-start(f32[72,128]{1,0:T(8,128)S(1)} %get-tuple-element.32.s0), channel_id=1, source_target_pairs={{0,32},{32,0},{64,96},{96,64},{1,33},{33,1},{65,97},{97,65},{2,34}... | collective-permute-start | bytes 110600 | tf_op jit(solution)/shard_map/ppermute | solution.py:478
  93.9 2.0 %image.1 = (f32[72,256]{1,0:T(8,128)S(1)}, f32[72,256]{1,0:T(8,128)S(1)}, f32[72,256]{1,0:T(8,128)S(1)}, f32[72,256]{1,0:T(8,128)S(1)}) custom-call(bf16[144,1024]{1,0:T(8,128)(2,1)S(1)} %get-tuple-element.35.left, bf16[256,1024]{1,0:T(8,128)(2,1)S(1)} %copy-done.2, bf16[256,1024]{1,0:T(8,128)(2,1)S(1)} %copy-done.3, bf16[512,1024]{1,0:T(8,128)(2,1)S(1)} %copy-done, ...), custom_call_target="tpu_custom_call" | custom-call | flops 1073741824 | bytes 5242880 | tf_op jit(solution)/shard_map/image/pallas_call | solution.py:364
  96.5 1.6 %collective-permute-start.12 = (f32[72,256]{1,0:T(8,128)S(1)}, f32[72,256]{1,0:T(8,128)S(1)}, u32[]{:S(2)}, u32[]{:S(2)}) collective-permute-start(f32[72,256]{1,0:T(8,128)S(1)} %get-tuple-element.45), channel_id=1, source_target_pairs={{0,96},{32,64},{64,32},{96,0},{1,97},{33,65},{65,33},{97,1},{2,98}... | collective-permute-start | bytes 221192 | tf_op jit(solution)/shard_map/ppermute | solution.py:478
  99.6 2.3 %collective-permute-done.8.s2 = f32[72,128]{1,0:T(8,128)S(1)} collective-permute-done((f32[72,128]{1,0:T(8,128)S(1)}, f32[72,128]{1,0:T(8,128)S(1)}, u32[]{:S(2)}, u32[]{:S(2)}) %collective-permute-start.8) | collective-permute-done | bytes 36896 | tf_op jit(solution)/shard_map/ppermute | solution.py:478
  101.8 1.5 %collective-permute-done.9.s3 = f32[72,128]{1,0:T(8,128)S(1)} collective-permute-done((f32[72,128]{1,0:T(8,128)S(1)}, f32[72,128]{1,0:T(8,128)S(1)}, u32[]{:S(2)}, u32[]{:S(2)}) %collective-permute-start.9) | collective-permute-done | bytes 36896 | tf_op jit(solution)/shard_map/ppermute | solution.py:478
  103.3 2.0 %shard_map.57 = (f32[64,128]{1,0:T(8,128)S(1)}, f32[8,128]{1,0:T(8,128)S(1)}) custom-call(f32[72,128]{1,0:T(8,128)S(1)} %get-tuple-element.32.s0, f32[72,128]{1,0:T(8,128)S(1)} %collective-permute-done.7.s1, f32[72,128]{1,0:T(8,128)S(1)} %collective-permute-done.8.s2, f32[72,128]{1,0:T(8,128)S(1)} %collective-permute-done.9.s3), custom_call_target="tpu_custom_call" | custom-call | tf_op jit(solution)/shard_map/pallas_call | solution.py:451
  107.0 1.1 collective-permute-start.15
  108.1 1.4 %shard_map.58 = f32[64,1024]{1,0:T(8,128)} custom-call(f32[1024,64]{1,0:T(8,128)S(1)} %get-tuple-element.31.tc, f32[64,128]{1,0:T(8,128)S(1)} %get-tuple-element.33.m, f32[8,128]{1,0:T(8,128)S(1)} %get-tuple-element.34.d), custom_call_target="tpu_custom_call" | custom-call | tf_op jit(solution)/shard_map/pallas_call | solution.py:451
  (43 shorter events, 8.3 us)
Async XLA Ops:
  0.6 8.9 %copy-start.4 = (bf16[3,32,512]{2,1,0:T(8,128)(2,1)S(1)}, bf16[3,32,512]{2,1,0:T(8,128)(2,1)}, u32[]{:S(2)}) copy-start(bf16[3,32,512]{2,1,0:T(8,128)(2,1)} %mine.1) | copy-start | bytes 294916
  0.6 22.6 %copy-start.5 = (f32[1024,64]{0,1:T(8,128)S(1)}, f32[1024,64]{0,1:T(8,128)}, u32[]{:S(2)}) copy-start(f32[1024,64]{0,1:T(8,128)} %param.5) | copy-start | bytes 786436
  0.6 8.9 %collective-permute-start = (bf16[3,32,512]{2,1,0:T(8,128)(2,1)}, bf16[3,32,512]{2,1,0:T(8,128)(2,1)S(1)}, u32[]{:S(2)}, u32[]{:S(2)}) collective-permute-start(bf16[3,32,512]{2,1,0:T(8,128)(2,1)} %mine.1), channel_id=1, source_target_pairs={{0,16},{1,17},{2,18},{3,19},{4,20},{5,21},{6,22},{7,23},{8,24},{9,... | collective-permute-start | bytes 294920 | tf_op jit(solution)/shard_map/ppermute | solution.py:474
  9.7 5.8 %collective-permute-start.1 = (bf16[3,64,512]{2,1,0:T(8,128)(2,1)S(1)}, bf16[3,64,512]{2,1,0:T(8,128)(2,1)S(1)}, u32[]{:S(2)}, u32[]{:S(2)}) collective-permute-start(bf16[3,64,512]{2,1,0:T(8,128)(2,1)S(1)} %shard_map.50.p0), channel_id=1, source_target_pairs={{0,1},{1,2},{2,3},{3,0},{4,5},{5,6},{6,7},{7,4},{8,9},{9,10},{10,1... | collective-permute-start | bytes 589832 | tf_op jit(solution)/shard_map/ppermute | solution.py:474
  11.0 4.5 %collective-permute-start.2 = (bf16[3,64,512]{2,1,0:T(8,128)(2,1)S(1)}, bf16[3,64,512]{2,1,0:T(8,128)(2,1)S(1)}, u32[]{:S(2)}, u32[]{:S(2)}) collective-permute-start(bf16[3,64,512]{2,1,0:T(8,128)(2,1)S(1)} %shard_map.50.p0), channel_id=1, source_target_pairs={{0,3},{1,0},{2,1},{3,2},{4,7},{5,4},{6,5},{7,6},{8,11},{9,8},{10,9... | collective-permute-start | bytes 589832 | tf_op jit(solution)/shard_map/ppermute | solution.py:474
  12.4 6.1 %collective-permute-start.3 = (bf16[3,64,512]{2,1,0:T(8,128)(2,1)S(1)}, bf16[3,64,512]{2,1,0:T(8,128)(2,1)S(1)}, u32[]{:S(2)}, u32[]{:S(2)}) collective-permute-start(bf16[3,64,512]{2,1,0:T(8,128)(2,1)S(1)} %shard_map.50.p0), channel_id=1, source_target_pairs={{0,2},{1,3},{2,0},{3,1},{4,6},{5,7},{6,4},{7,5},{8,10},{9,11},{10,... | collective-permute-start | bytes 589832 | tf_op jit(solution)/shard_map/ppermute | solution.py:474
  19.5 14.8 %collective-permute-start.6 = (bf16[3,256,512]{2,1,0:T(8,128)(2,1)}, bf16[3,256,512]{2,1,0:T(8,128)(2,1)S(1)}, u32[]{:S(2)}, u32[]{:S(2)}) collective-permute-start(bf16[3,256,512]{2,1,0:T(8,128)(2,1)} %get-tuple-element.28), channel_id=1, source_target_pairs={{0,8},{1,9},{2,10},{3,11},{4,12},{5,13},{6,14},{7,15},{8,0},{9,1},... | collective-permute-start | bytes 2359304 | tf_op jit(solution)/shard_map/ppermute | solution.py:474
  23.3 19.1 %collective-permute-start.4 = (bf16[3,256,512]{2,1,0:T(8,128)(2,1)}, bf16[3,256,512]{2,1,0:T(8,128)(2,1)S(1)}, u32[]{:S(2)}, u32[]{:S(2)}) collective-permute-start(bf16[3,256,512]{2,1,0:T(8,128)(2,1)} %get-tuple-element.28), channel_id=1, source_target_pairs={{0,4},{1,5},{2,6},{3,7},{4,8},{5,9},{6,10},{7,11},{8,12},{9,13},{1... | collective-permute-start | bytes 2359304 | tf_op jit(solution)/shard_map/ppermute | solution.py:474
  24.4 18.2 %collective-permute-start.5 = (bf16[3,256,512]{2,1,0:T(8,128)(2,1)}, bf16[3,256,512]{2,1,0:T(8,128)(2,1)S(1)}, u32[]{:S(2)}, u32[]{:S(2)}) collective-permute-start(bf16[3,256,512]{2,1,0:T(8,128)(2,1)} %get-tuple-element.28), channel_id=1, source_target_pairs={{0,12},{1,13},{2,14},{3,15},{4,0},{5,1},{6,2},{7,3},{8,4},{9,5},{1... | collective-permute-start | bytes 2359304 | tf_op jit(solution)/shard_map/ppermute | solution.py:474
  57.2 36.7 %copy-start = (bf16[512,1024]{1,0:T(8,128)(2,1)S(1)}, bf16[512,1024]{1,0:T(8,128)(2,1)}, u32[]{:S(2)}) copy-start(bf16[512,1024]{1,0:T(8,128)(2,1)} %get-tuple-element.38.h1) | copy-start | bytes 3145732
  57.2 36.7 %copy-start.1 = (bf16[512,1024]{1,0:T(8,128)(2,1)S(1)}, bf16[512,1024]{1,0:T(8,128)(2,1)}, u32[]{:S(2)}) copy-start(bf16[512,1024]{1,0:T(8,128)(2,1)} %get-tuple-element.39.l1) | copy-start | bytes 3145732
  57.2 36.7 %copy-start.2 = (bf16[256,1024]{1,0:T(8,128)(2,1)S(1)}, bf16[256,1024]{1,0:T(8,128)(2,1)}, u32[]{:S(2)}) copy-start(bf16[256,1024]{1,0:T(8,128)(2,1)} %get-tuple-element.36.h0) | copy-start | bytes 1572868
  57.2 36.7 %copy-start.3 = (bf16[256,1024]{1,0:T(8,128)(2,1)S(1)}, bf16[256,1024]{1,0:T(8,128)(2,1)}, u32[]{:S(2)}) copy-start(bf16[256,1024]{1,0:T(8,128)(2,1)} %get-tuple-element.37.l0) | copy-start | bytes 1572868
  87.4 11.2 %collective-permute-start.7 = (f32[72,128]{1,0:T(8,128)S(1)}, f32[72,128]{1,0:T(8,128)S(1)}, u32[]{:S(2)}, u32[]{:S(2)}) collective-permute-start(f32[72,128]{1,0:T(8,128)S(1)} %get-tuple-element.32.s0), channel_id=1, source_target_pairs={{0,32},{32,0},{64,96},{96,64},{1,33},{33,1},{65,97},{97,65},{2,34}... | collective-permute-start | bytes 110600 | tf_op jit(solution)/shard_map/ppermute | solution.py:478
  95.9 9.4 %collective-permute-start.10 = (f32[72,256]{1,0:T(8,128)S(1)}, f32[72,256]{1,0:T(8,128)S(1)}, u32[]{:S(2)}, u32[]{:S(2)}) collective-permute-start(f32[72,256]{1,0:T(8,128)S(1)} %get-tuple-element.43), channel_id=1, source_target_pairs={{0,32},{32,0},{64,96},{96,64},{1,33},{33,1},{65,97},{97,65},{2,34}... | collective-permute-start | bytes 221192 | tf_op jit(solution)/shard_map/ppermute | solution.py:478
  96.0 9.3 %collective-permute-start.11 = (f32[72,256]{1,0:T(8,128)S(1)}, f32[72,256]{1,0:T(8,128)S(1)}, u32[]{:S(2)}, u32[]{:S(2)}) collective-permute-start(f32[72,256]{1,0:T(8,128)S(1)} %get-tuple-element.44), channel_id=1, source_target_pairs={{0,64},{32,96},{64,0},{96,32},{1,65},{33,97},{65,1},{97,33},{2,66}... | collective-permute-start | bytes 221192 | tf_op jit(solution)/shard_map/ppermute | solution.py:478
  96.5 8.8 %collective-permute-start.12 = (f32[72,256]{1,0:T(8,128)S(1)}, f32[72,256]{1,0:T(8,128)S(1)}, u32[]{:S(2)}, u32[]{:S(2)}) collective-permute-start(f32[72,256]{1,0:T(8,128)S(1)} %get-tuple-element.45), channel_id=1, source_target_pairs={{0,96},{32,64},{64,32},{96,0},{1,97},{33,65},{65,33},{97,1},{2,98}... | collective-permute-start | bytes 221192 | tf_op jit(solution)/shard_map/ppermute | solution.py:478
  98.1 3.7 %collective-permute-start.8 = (f32[72,128]{1,0:T(8,128)S(1)}, f32[72,128]{1,0:T(8,128)S(1)}, u32[]{:S(2)}, u32[]{:S(2)}) collective-permute-start(f32[72,128]{1,0:T(8,128)S(1)} %get-tuple-element.32.s0), channel_id=1, source_target_pairs={{0,64},{32,96},{64,0},{96,32},{1,65},{33,97},{65,1},{97,33},{2,66}... | collective-permute-start | bytes 110600 | tf_op jit(solution)/shard_map/ppermute | solution.py:478
  98.5 4.8 %collective-permute-start.9 = (f32[72,128]{1,0:T(8,128)S(1)}, f32[72,128]{1,0:T(8,128)S(1)}, u32[]{:S(2)}, u32[]{:S(2)}) collective-permute-start(f32[72,128]{1,0:T(8,128)S(1)} %get-tuple-element.32.s0), channel_id=1, source_target_pairs={{0,96},{32,64},{64,32},{96,0},{1,97},{33,65},{65,33},{97,1},{2,98}... | collective-permute-start | bytes 110600 | tf_op jit(solution)/shard_map/ppermute | solution.py:478
  105.9 3.6 %collective-permute-start.13 = (bf16[64,256]{1,0:T(8,128)(2,1)S(1)}, bf16[64,256]{1,0:T(8,128)(2,1)S(1)}, u32[]{:S(2)}, u32[]{:S(2)}) collective-permute-start(bf16[64,256]{1,0:T(8,128)(2,1)S(1)} %shard_map.59.i0), channel_id=1, source_target_pairs={{0,32},{32,0},{64,96},{96,64},{1,33},{33,1},{65,97},{97,65},{2,34}... | collective-permute-start | bytes 98312 | tf_op jit(solution)/shard_map/ppermute | solution.py:478
  106.3 3.3 %collective-permute-start.14 = (bf16[64,256]{1,0:T(8,128)(2,1)S(1)}, bf16[64,256]{1,0:T(8,128)(2,1)S(1)}, u32[]{:S(2)}, u32[]{:S(2)}) collective-permute-start(bf16[64,256]{1,0:T(8,128)(2,1)S(1)} %shard_map.59.i0), channel_id=1, source_target_pairs={{0,64},{32,96},{64,0},{96,32},{1,65},{33,97},{65,1},{97,33},{2,66}... | collective-permute-start | bytes 98312 | tf_op jit(solution)/shard_map/ppermute | solution.py:478
  107.0 3.4 %collective-permute-start.15 = (bf16[64,256]{1,0:T(8,128)(2,1)S(1)}, bf16[64,256]{1,0:T(8,128)(2,1)S(1)}, u32[]{:S(2)}, u32[]{:S(2)}) collective-permute-start(bf16[64,256]{1,0:T(8,128)(2,1)S(1)} %shard_map.59.i0), channel_id=1, source_target_pairs={{0,96},{32,64},{64,32},{96,0},{1,97},{33,65},{65,33},{97,1},{2,98}... | collective-permute-start | bytes 98312 | tf_op jit(solution)/shard_map/ppermute | solution.py:478
